TPU v7x, 256 devices: a whole 4x4x8 slice. The times are simulated.
256 devices in a mesh: grp: 8 (over z), tp: 32 (over x, y, core).
Axes of the slice: x: 4, y: 4, z: 8, core: 2. Of those that a mesh axis runs over, the one named last changes fastest.
Arguments:
- hidden_in: bfloat16 [1024, 3584], P(('grp', 'tp')), may hold values from -6 to 6
- norm_gains: float32 [4, 3584], replicated, may hold values from 0.25 to 1.75
- w_qkv: bfloat16 [3584, 8192], P(None, 'tp'), may hold values from -0.09375 to 0.09375
- w_out: bfloat16 [4096, 3584], P('tp'), may hold values from -0.09375 to 0.09375
- w_gate_up: bfloat16 [2, 3584, 8192], P(None, None, 'tp'), may hold values from -0.09375 to 0.09375
- w_down: bfloat16 [8192, 3584], P('tp'), may hold values from -0.0625 to 0.0625
- prompt_keys: bfloat16 [32768, 2048], P(('grp', 'tp')), may hold values from -480 to 480, as said below
- prompt_values: bfloat16 [32768, 2048], P(('grp', 'tp')), may hold values from -6 to 6
- tail_keys: bfloat16 [1024, 64, 2048], P(('grp', 'tp')), may hold values from -480 to 480, as said below
- tail_values: bfloat16 [1024, 64, 2048], P(('grp', 'tp')), may hold values from -6 to 6
- prompt_len: int32 [80], replicated, may hold values from 1 to 4087, as said below
- group_home: int32 [80], replicated, may hold values from 0 to 7, as said below
- req_group: int32 [1024], P('grp'), may hold values from 0 to 79, as said below
- tail_len: int32 [1024], P('grp'), may hold values from 1 to 64, 32768 in all
Outputs:
- layer_out: bfloat16 [1024, 3584], P(('grp', 'tp'))
Inputs may be any that keep to these rules, and one draw needn't show every extreme that they name: `group_home`: each grp device is home to exactly 10 groups. `prompt_len`: the prompts of the groups homed on one grp device lie one after another in order of group id from the first of that device's 4096 cache positions; together they hold at most 4096 positions, exactly 4096 on one home in every draw, where one group holds 4087 of them. `req_group`: of the 128 requests held by one grp device, at most 32 belong to groups homed on any one grp device; in every draw one home receives exactly 32 requests from every grp device. `prompt_keys`: cached keys, already rotated. `tail_keys`: cached keys, already rotated.
All inputs are finite; a program needn't handle non-finite values. No bound on the sum of `tail_len` on one device may be relied on, other than what follows from the above.
Results may differ from a plain program's by a relative error of at most 0.015.
Values may be sent and summed in bfloat16 or wider, within the bound.
A program may use at most 128 MiB of HBM per device.

v0:
```python
import math
import jax
import jax.numpy as jnp
from jax import lax
from jax.sharding import PartitionSpec as P

HEADS = 16
KV_HEADS = 8
HEAD_DIM = 256
NORM_EPS = 1e-06
SOFT_CAP = 50.0


def rms_scale(values, gain_row):
    values = values.astype(jnp.float32)
    return (
        values * lax.rsqrt(jnp.mean(values * values, axis=-1, keepdims=True) + NORM_EPS) * gain_row
    )


def rotate(head_rows, position):
    half_width = head_rows.shape[-1] // 2
    freq_index = jnp.arange(half_width).astype(jnp.float32)
    frequency = jnp.exp(freq_index * (-math.log(10000.0) / half_width))
    angles = position.astype(jnp.float32)[:, None] * frequency[None, :]
    cosine = jnp.cos(angles)[:, None, :]
    sine_part = jnp.sin(angles)[:, None, :]
    head_rows = head_rows.astype(jnp.float32)
    first_half = head_rows[..., :half_width]
    second = head_rows[..., half_width:]
    return jnp.concatenate(
        [first_half * cosine - second * sine_part, second * cosine + first_half * sine_part],
        axis=-1,
    )


def capped(scores):
    return SOFT_CAP * jnp.tanh(scores * HEAD_DIM ** (-0.5) / SOFT_CAP)


def lookup(lookup_table, index_list):
    matches = index_list[:, None] == jnp.arange(lookup_table.shape[0], dtype=jnp.int32)[None, :]
    return jnp.sum(jnp.where(matches, lookup_table[None, :], 0), axis=1)


def group_starts(prompt_len, group_home):
    group_ids = jnp.arange(prompt_len.shape[0], dtype=jnp.int32)
    same_home = group_home[:, None] == group_home[None, :]
    earlier = group_ids[None, :] < group_ids[:, None]
    return jnp.sum(jnp.where(same_home & earlier, prompt_len[None, :], 0), axis=1)


def shared_part(queries, key_rows, value_rows, visible):
    scores = capped(
        jnp.einsum("nkjd,pkd->nkjp", queries, key_rows, preferred_element_type=jnp.float32)
    )
    exponent = jnp.where(visible[:, None, None, :], jnp.exp(scores), 0.0)
    numerator = jnp.einsum(
        "nkjp,pkd->nkjd",
        exponent.astype(jnp.bfloat16),
        value_rows,
        preferred_element_type=jnp.float32,
    )
    return (numerator, jnp.sum(exponent, axis=-1))


def own_part(queries, key_rows, value_rows, visible):
    scores = capped(
        jnp.einsum("nkjd,npkd->nkjp", queries, key_rows, preferred_element_type=jnp.float32)
    )
    exponent = jnp.where(visible[:, None, None, :], jnp.exp(scores), 0.0)
    numerator = jnp.einsum(
        "nkjp,npkd->nkjd",
        exponent.astype(jnp.bfloat16),
        value_rows,
        preferred_element_type=jnp.float32,
    )
    return (numerator, jnp.sum(exponent, axis=-1))


def per_device(
    hidden_in,
    norm_gains,
    w_qkv,
    w_out,
    w_gate_up,
    w_down,
    prompt_keys,
    prompt_values,
    tail_keys,
    tail_values,
    prompt_len,
    group_home,
    req_group,
    tail_len,
):
    tp_rank = lax.axis_index("tp")
    q_width = HEADS * HEAD_DIM
    kv_width = KV_HEADS * HEAD_DIM
    row_count = hidden_in.shape[0]
    normed = rms_scale(hidden_in, norm_gains[0]).astype(jnp.bfloat16)
    qkv_share = jnp.dot(
        lax.all_gather(normed, "tp", axis=0, tiled=True), w_qkv, preferred_element_type=jnp.float32
    ).astype(jnp.bfloat16)
    projected_qkv = lax.all_gather(qkv_share, "tp", axis=1, tiled=True)
    requests = projected_qkv.shape[0]
    req_len = lookup(prompt_len, req_group)
    position = req_len + tail_len
    queries = rotate(
        projected_qkv[:, :q_width].reshape(requests, HEADS, HEAD_DIM), position
    ).astype(jnp.bfloat16)
    queries = queries.reshape(requests, KV_HEADS, 2, HEAD_DIM)
    key_new = rotate(
        projected_qkv[:, q_width : q_width + kv_width].reshape(requests, KV_HEADS, HEAD_DIM),
        position,
    ).astype(jnp.bfloat16)
    value_new = projected_qkv[:, q_width + kv_width :].reshape(requests, KV_HEADS, HEAD_DIM)
    starts = group_starts(prompt_len, group_home)
    req_home = lookup(group_home, req_group)
    req_start = lookup(starts, req_group)
    cap_dev = prompt_keys.shape[0]
    row_first = tp_rank * row_count
    own_queries = lax.dynamic_slice_in_dim(queries, row_first, row_count, 0)
    own_tail_len = lax.dynamic_slice_in_dim(tail_len, row_first, row_count, 0)
    tail_dev = tail_keys.shape[1]
    tail_pos = jnp.arange(tail_dev, dtype=jnp.int32)
    own_num, own_den = own_part(
        own_queries,
        tail_keys.reshape(row_count, tail_dev, KV_HEADS, HEAD_DIM),
        tail_values.reshape(row_count, tail_dev, KV_HEADS, HEAD_DIM),
        tail_pos[None, :] < own_tail_len[:, None],
    )
    numerator = lax.dynamic_update_slice_in_dim(
        jnp.zeros((requests, KV_HEADS, 2, HEAD_DIM), jnp.float32), own_num, row_first, 0
    )
    denominator = lax.dynamic_update_slice_in_dim(
        jnp.zeros((requests, KV_HEADS, 2), jnp.float32), own_den, row_first, 0
    )
    key_piece = lax.all_gather(prompt_keys, "grp", axis=0, tiled=True)
    value_piece = lax.all_gather(prompt_values, "grp", axis=0, tiled=True)
    piece_rows = key_piece.shape[0]
    gathered_index = jnp.arange(piece_rows, dtype=jnp.int32)
    home_index = gathered_index // cap_dev
    piece_offsets = tp_rank * cap_dev + gathered_index % cap_dev
    visible = (
        (home_index[None, :] == req_home[:, None])
        & (piece_offsets[None, :] >= req_start[:, None])
        & (piece_offsets[None, :] < (req_start + req_len)[:, None])
    )
    part_num, part_den = shared_part(
        queries,
        key_piece.reshape(piece_rows, KV_HEADS, HEAD_DIM),
        value_piece.reshape(piece_rows, KV_HEADS, HEAD_DIM),
        visible,
    )
    numerator, denominator = (numerator + part_num, denominator + part_den)
    share_width = w_out.shape[0]
    first_col = tp_rank * share_width
    flat_num = numerator.reshape(requests, q_width)
    flat_den = denominator.reshape(requests, HEADS)
    total_num, total_den = lax.psum((flat_num, flat_den), "tp")
    share_num = lax.dynamic_slice_in_dim(total_num, first_col, share_width, 1)
    self_exp = jnp.exp(
        capped(jnp.einsum("nkjd,nkd->nkj", queries, key_new, preferred_element_type=jnp.float32))
    )
    self_num = (
        lax.optimization_barrier(self_exp.astype(jnp.bfloat16)).astype(jnp.float32)[..., None]
        * value_new.astype(jnp.float32)[:, :, None, :]
    )
    self_share = lax.dynamic_slice_in_dim(
        self_num.reshape(requests, q_width), first_col, share_width, 1
    )
    total_den = total_den + self_exp.reshape(requests, HEADS)
    head_of_col = (first_col + jnp.arange(share_width, dtype=jnp.int32)) // HEAD_DIM
    head_pick = (head_of_col[None, :] == jnp.arange(HEADS, dtype=jnp.int32)[:, None]).astype(
        jnp.float32
    )
    den_cols = jnp.dot(total_den, head_pick, precision=lax.Precision.HIGHEST)
    attn_share = ((share_num + self_share) / den_cols).astype(jnp.bfloat16)
    block_rows = attn_share
    attn_proj = lax.psum_scatter(
        jnp.dot(block_rows, w_out, preferred_element_type=jnp.float32),
        "tp",
        scatter_dimension=0,
        tiled=True,
    )
    resid = (hidden_in.astype(jnp.float32) + rms_scale(attn_proj, norm_gains[1])).astype(
        jnp.bfloat16
    )
    ffn_in = rms_scale(resid, norm_gains[2]).astype(jnp.bfloat16)
    gate_up = jnp.einsum(
        "rd,kdf->krf",
        lax.all_gather(ffn_in, "tp", axis=0, tiled=True),
        w_gate_up,
        preferred_element_type=jnp.float32,
    )
    hidden_units = (jax.nn.gelu(gate_up[0], approximate=True) * gate_up[1]).astype(jnp.bfloat16)
    block_rows = hidden_units
    ffn_proj = lax.psum_scatter(
        jnp.dot(block_rows, w_down, preferred_element_type=jnp.float32).astype(jnp.bfloat16),
        "tp",
        scatter_dimension=0,
        tiled=True,
    ).astype(jnp.float32)
    return (resid.astype(jnp.float32) + rms_scale(ffn_proj, norm_gains[3])).astype(jnp.bfloat16)


def solution(mesh):
    in_specs = (
        P(("grp", "tp"), None),
        P(),
        P(None, "tp"),
        P("tp", None),
        P(None, None, "tp"),
        P("tp", None),
        P(("grp", "tp"), None),
        P(("grp", "tp"), None),
        P(("grp", "tp"), None, None),
        P(("grp", "tp"), None, None),
        P(),
        P(),
        P("grp"),
        P("grp"),
    )
    out_specs = P(("grp", "tp"), None)
    return jax.shard_map(
        per_device, mesh=mesh, in_specs=in_specs, out_specs=out_specs, check_vma=False
    )
```

profile of v0, /device:TPU:1, one launch (start us, length us, event | category | flops | bytes accessed | tf_op | source)
XLA Modules:
  0.0 625.6 jit_solution(4266515688802575155)
XLA Ops:
  6.5 1.2 slice_reduce_fusion.1
  9.5 26.6 %all-gather = bf16[32,4,3584]{2,1,0:T(4,128)(2,1)S(1)} all-gather(bf16[1,4,3584]{2,1,0:T(4,128)(2,1)S(1)} %fusion.47), channel_id=1, replica_groups=mesh['grp'=8,'tp'=32] {'tp'}, dimensions={0}, use_global_device_ids=true | all-gather | bytes 946176 | tf_op jit(solution)/shard_map/all_gather | solution.py:103
  36.0 1.1 reshape.279
  37.2 2.9 convolution_convert_fusion.1
  44.0 46.5 %all-gather.6.cloned.1.call-done = bf16[128,8192]{1,0:T(8,128)(2,1)} async-done(((bf16[128,256]{1,0:T(8,128)(2,1)}), bf16[128,8192]{1,0:T(8,128)(2,1)}) %all-gather.6.cloned.1.call-update) | async-done | bytes 2097168 | tf_op jit(solution)/shard_map/all_gather | solution.py:105
  90.5 1.4 slice_convert_fusion
  94.7 2.4 slice_convert_fusion.2
  97.8 1.2 pad_maximum_fusion
  99.2 50.9 %all-gather.8.cloned.1.call-done = bf16[1024,2048]{0,1:T(8,128)(2,1)} async-done(((bf16[128,2048]{0,1:T(8,128)(2,1)}), bf16[1024,2048]{0,1:T(8,128)(2,1)}) %all-gather.8.cloned.1.call-update) | async-done | bytes 4194320 | tf_op jit(solution)/shard_map/all_gather | solution.py:139
  150.1 7.7 %bitcast_reduce_fusion = (f32[128,8,2]{0,2,1:T(2,128)S(1)}, f32[8,128,2,1024]{3,1,2,0:T(8,128)}) fusion(pred[128,1024]{1,0:T(8,128)(4,1)} %compare_and_fusion, bf16[1024,8,256,1]{0,2,3,1:T(8,128)(2,1)} %bitcast.96, bf16[128,8,2,128]{3,0,2,1:T(8,128)(2,1)S(1)} %bitcast.87, bf16[128,8,2,128]{3,0,2,1:T(8,128)(2,1)S(1)} %bitcast.84), kind=kOutput, calls=%fused_computation | convolution fusion | flops 1084225536 | bytes 13770752 | tf_op jit(solution)/shard_map/nkjd,pkd->nkjp/dot_general | solution.py:55
  157.8 55.1 %all-gather.10.cloned.1.call-done = bf16[1024,2048]{0,1:T(8,128)(2,1)} async-done(((bf16[128,2048]{0,1:T(8,128)(2,1)}), bf16[1024,2048]{0,1:T(8,128)(2,1)}) %all-gather.10.cloned.1.call-update) | async-done | bytes 4194320 | tf_op jit(solution)/shard_map/all_gather | solution.py:140
  212.9 7.0 %fusion = f32[8,128,2,256]{3,1,2,0:T(8,128)S(1)} fusion(bf16[1024,8,256,1]{0,2,3,1:T(8,128)(2,1)} %bitcast.97, f32[8,128,2,1024]{3,1,2,0:T(8,128)} %get-tuple-element.27, pred[128,1024]{1,0:T(8,128)(4,1)} %compare_and_fusion), kind=kOutput, calls=%fused_computation.4 | convolution fusion | flops 1082130432 | bytes 14811136 | tf_op jit(solution)/shard_map/nkjp,pkd->nkjd/dot_general | solution.py:58
  220.0 1.4 copy.123
  222.0 2.9 copy.85
  224.9 2.9 copy.86
  228.1 3.4 fusion.15
  231.4 1.2 copy.94
  233.3 2.8 broadcast_multiply_fusion
  236.1 4.0 mul.269
  240.2 1.3 add.147
  241.4 67.5 %psum.15 = f32[128,16]{0,1:T(8,128)S(1)} all-reduce(f32[128,16]{0,1:T(8,128)S(1)} %bitcast.94), channel_id=1, replica_groups=mesh['grp'=8,'tp'=32] {'tp'}, use_global_device_ids=true, to_apply=%region_8.9 | all-reduce | flops 2048 | bytes 16384 | tf_op jit(solution)/shard_map/psum | solution.py:161
  309.0 38.9 %all-reduce.6.cloned.1.call-done = f32[128,4096]{1,0:T(8,128)} async-done(((f32[128,4096]{1,0:T(8,128)}), f32[128,4096]{1,0:T(8,128)}) %all-reduce.6.cloned.1.call-update) | async-done | bytes 2097168 | tf_op jit(solution)/shard_map/psum | solution.py:161
  347.9 1.1 fusion.5
  349.1 1.6 fusion.74
  352.0 115.3 %all-reduce.8.cloned.1.call-done = f32[128,3584]{1,0:T(8,128)} async-done(((f32[128,3584]{1,0:T(8,128)}), f32[128,3584]{1,0:T(8,128)}) %all-reduce.8.cloned.1.call-update) | async-done | bytes 1835024
  468.4 1.1 fusion.39
  469.6 28.2 %all-gather.1 = bf16[32,4,3584]{2,1,0:T(4,128)(2,1)} all-gather(bf16[1,4,3584]{2,1,0:T(4,128)(2,1)S(1)} %fusion.46), channel_id=1, replica_groups=mesh['grp'=8,'tp'=32] {'tp'}, dimensions={0}, use_global_device_ids=true | all-gather | bytes 946176 | tf_op jit(solution)/shard_map/all_gather | solution.py:193
  497.9 1.7 reshape.286
  499.5 2.7 convolution_bitcast_fusion
  502.2 1.4 convolution_convert_fusion
  503.7 112.7 %all-reduce.10.cloned.1.call-done = bf16[128,3584]{1,0:T(8,128)(2,1)} async-done(((bf16[128,3584]{1,0:T(8,128)(2,1)}), bf16[128,3584]{1,0:T(8,128)(2,1)}) %all-reduce.10.cloned.1.call-update) | async-done | bytes 917520
  617.3 1.5 fusion.42
  (77 shorter events, 13.6 us)
Async XLA Ops:
  6.5 495.7 %copy-start = (bf16[256,3584]{1,0:T(8,128)(2,1)S(1)}, bf16[256,3584]{1,0:T(8,128)(2,1)}, u32[]{:S(2)}) copy-start(bf16[256,3584]{1,0:T(8,128)(2,1)} %param.19) | copy-start | bytes 5505028
  6.5 83.9 %all-gather.6.cloned.1.call-start = ((), (), s32[]{:S(2)}) async-start(), calls=%async_computation | async-start | bytes 2162688 | tf_op jit(solution)/shard_map/all_gather | solution.py:105
  36.0 4.1 copy-start.4
  37.2 4.0 copy-start.5
  40.0 2.3 copy-start.10
  40.1 2.4 copy-start.7
  40.1 2.4 copy-start.8
  40.1 2.6 copy-start.9
  40.1 110.0 %all-gather.8.cloned.1.call-start = ((), (), s32[]{:S(2)}) async-start(), calls=%async_computation.1 | async-start | bytes 4718592 | tf_op jit(solution)/shard_map/all_gather | solution.py:139
  41.2 171.8 %all-gather.10.cloned.1.call-start = ((), (), s32[]{:S(2)}) async-start(), calls=%async_computation.2 | async-start | bytes 4718592 | tf_op jit(solution)/shard_map/all_gather | solution.py:140
  42.3 305.7 %all-reduce.6.cloned.1.call-start = ((), (), s32[]{:S(2)}) async-start(), calls=%async_computation.3 | async-start | bytes 4194304 | tf_op jit(solution)/shard_map/psum | solution.py:161
  92.9 1.2 copy-start.11
  97.5 1.4 copy-start.2
  227.8 5.1 copy-start.1
  227.8 239.5 %all-reduce.8.cloned.1.call-start = ((), (), s32[]{:S(2)}) async-start(), calls=%async_computation.4 | async-start | bytes 3670016
  236.1 113.0 %copy-start.3 = (bf16[128,3584]{1,0:T(8,128)(2,1)S(1)}, bf16[128,3584]{1,0:T(8,128)(2,1)}, u32[]{:S(2)}) copy-start(bf16[128,3584]{1,0:T(8,128)(2,1)} %param.17) | copy-start | bytes 2752516
  349.1 1.7 copy-start.12
  349.1 119.3 %copy-start.6 = (bf16[4,3584]{1,0:T(4,128)(2,1)S(1)}, bf16[4,3584]{1,0:T(4,128)(2,1)}, u32[]{:S(2)}) copy-start(bf16[4,3584]{1,0:T(4,128)(2,1)} %param.14) | copy-start | bytes 86020
  350.7 265.6 %all-reduce.10.cloned.1.call-start = ((), (), s32[]{:S(2)}) async-start(), calls=%async_computation.5 | async-start | bytes 1835008
Sparse Core Ops, SparseCore 0:
  40.2 50.2 all-gather.5
  92.2 57.8 all-gather.7
  151.8 61.1 all-gather.9
  228.0 119.9 all-reduce.5
  351.1 116.2 all-reduce.7
  503.8 112.4 all-reduce.9
where the time goes:
time: 626 us
  waiting for transfers between devices  419 us (67%)
  blocking collectives  122 us (19%)
  matrix products  28.5 us (5%)
  local copies, waits for them, and re-layouts  23.3 us (4%)
  other arithmetic  17.2 us (3%)
  between operations  14.4 us (2%)
    unnamed x8, waiting for transfers between devices  228 us
    psum x1, blocking collectives, per_device(): total_num, total_den = lax.psum((flat_num, flat_den), 'tp')  67.5 us
    all_gather x1, waiting for transfers between devices, per_device(): value_piece = lax.all_gather(prompt_values, 'grp', axis=0, tiled=True)  55.1 us
    all_gather x1, waiting for transfers between devices, per_device(): key_piece = lax.all_gather(prompt_keys, 'grp', axis=0, tiled=True)  50.9 us
    all_gather x1, waiting for transfers between devices, per_device(): projected_qkv = lax.all_gather(qkv_share, 'tp', axis=1, tiled=True)  46.5 us
    psum x1, waiting for transfers between devices, per_device(): total_num, total_den = lax.psum((flat_num, flat_den), 'tp')  38.9 us
    all_gather x1, blocking collectives, per_device(): lax.all_gather(ffn_in, 'tp', axis=0, tiled=True)  28.2 us
    all_gather x1, blocking collectives, per_device(): lax.all_gather(normed, 'tp', axis=0, tiled=True)  26.6 us
  transfers between devices with their start and end apart: 6, of which 6 were waited for; matrix products, arithmetic and copies ran while one was open for 5% of the time, Pallas kernels for 0%

commit v1 on v0

--- a/solution.py
+++ b/solution.py
@@ -9,6 +9,11 @@
 HEAD_DIM = 256
 NORM_EPS = 1e-06
 SOFT_CAP = 50.0
+
+
+def gather_from_all(x, axis, dim):
+    copies = jnp.concatenate([x] * lax.axis_size(axis), axis=dim)
+    return lax.all_to_all(copies, axis, dim, dim, tiled=True)
 
 
 def rms_scale(values, gain_row):
@@ -136,7 +141,7 @@
     denominator = lax.dynamic_update_slice_in_dim(
         jnp.zeros((requests, KV_HEADS, 2), jnp.float32), own_den, row_first, 0
     )
-    key_piece = lax.all_gather(prompt_keys, "grp", axis=0, tiled=True)
+    key_piece = gather_from_all(prompt_keys, "grp", 0)
     value_piece = lax.all_gather(prompt_values, "grp", axis=0, tiled=True)
     piece_rows = key_piece.shape[0]
     gathered_index = jnp.arange(piece_rows, dtype=jnp.int32)

time: 626 us -> 598 us (0.955)
  waiting for transfers between devices: 419 us -> 383 us
  starting transfers between devices: 0.39 us -> 8.89 us
    all_to_all x0 -> x1, waiting for transfers between devices: none -> 62.2 us  [gather_from_all(): return lax.all_to_all(copies, axis, dim, dim, tiled=True)]
    all_gather x1 -> x0, waiting for transfers between devices: 50.9 us -> none  [per_device(): key_piece = lax.all_gather(prompt_keys, 'grp', axis=0, tiled=True)]
    all_gather x1, waiting for transfers between devices: 55.1 us -> 18.5 us  [per_device(): value_piece = lax.all_gather(prompt_values, 'grp', axis=0, tiled=True)]
    all_gather x1, waiting for transfers between devices: 46.5 us -> 36.5 us  [per_device(): projected_qkv = lax.all_gather(qkv_share, 'tp', axis=1, tiled=True)]
    all_to_all x0 -> x1, starting transfers between devices: none -> 8.33 us  [gather_from_all(): return lax.all_to_all(copies, axis, dim, dim, tiled=True)]
    unnamed x35 -> x46, local copies, waits for them, and re-layouts: 9.03 us -> 13.7 us
    unnamed x8 -> x7, waiting for transfers between devices: 228 us -> 228 us
  transfers between devices with their start and end apart: 6 -> 6, of which waited for: 6 -> 6; matrix products, arithmetic and copies ran while one was open for 5% -> 6% of each run, Pallas kernels for 0% -> 0%
where the time goes in v1:
time: 598 us; the launch traced here: 597 us
  waiting for transfers between devices  383 us (64%)
  blocking collectives  119 us (20%)
  local copies, waits for them, and re-layouts  28 us (5%)
  matrix products  26 us (4%)
  other arithmetic  17.3 us (3%)
  between operations  14.2 us (2%)
  starting transfers between devices  8.89 us (1%)
    unnamed x7, waiting for transfers between devices  228 us
    psum x1, blocking collectives, per_device(): total_num, total_den = lax.psum((flat_num, flat_den), 'tp')  64.7 us
    all_to_all x1, waiting for transfers between devices, gather_from_all(): return lax.all_to_all(copies, axis, dim, dim, tiled=True)  62.2 us
    psum x1, waiting for transfers between devices, per_device(): total_num, total_den = lax.psum((flat_num, flat_den), 'tp')  37.9 us
    all_gather x1, waiting for transfers between devices, per_device(): projected_qkv = lax.all_gather(qkv_share, 'tp', axis=1, tiled=True)  36.5 us
    all_gather x1, blocking collectives, per_device(): lax.all_gather(ffn_in, 'tp', axis=0, tiled=True)  28.2 us
    all_gather x1, blocking collectives, per_device(): lax.all_gather(normed, 'tp', axis=0, tiled=True)  26.6 us
    all_gather x1, waiting for transfers between devices, per_device(): value_piece = lax.all_gather(prompt_values, 'grp', axis=0, tiled=True)  18.5 us
  transfers between devices with their start and end apart: 6, of which 6 were waited for; matrix products, arithmetic and copies ran while one was open for 6% of the time, Pallas kernels for 0%

profile of v1, /device:TPU:1, one launch (start us, length us, event | category | flops | bytes accessed | tf_op | source)
XLA Modules:
  0.0 597.0 jit_solution(4218699757436684468)
XLA Ops:
  6.5 1.2 slice_reduce_fusion.1
  9.5 26.6 %all-gather = bf16[32,4,3584]{2,1,0:T(4,128)(2,1)S(1)} all-gather(bf16[1,4,3584]{2,1,0:T(4,128)(2,1)S(1)} %fusion.52), channel_id=1, replica_groups=mesh['grp'=8,'tp'=32] {'tp'}, dimensions={0}, use_global_device_ids=true | all-gather | bytes 946176 | tf_op jit(solution)/shard_map/all_gather | solution.py:108
  37.2 2.8 convolution_convert_fusion.1
  40.5 2.0 copy-done.2
  42.4 8.3 %all-to-all-start = ((bf16[8,128,2048]{2,1,0:T(8,128)(2,1)}), bf16[8,128,2048]{2,1,0:T(8,128)(2,1)}, u32[]{:S(2)}, u32[]{:S(2)}) async-start(bf16[8,128,2048]{2,1,0:T(8,128)(2,1)} %bitcast.85), calls=%async_computation | async-start | bytes 8388608 | tf_op jit(solution)/shard_map/all_to_all | solution.py:16
  53.9 36.5 %all-gather.5.cloned.1.call-done = bf16[128,8192]{1,0:T(8,128)(2,1)} async-done(((bf16[128,256]{1,0:T(8,128)(2,1)}), bf16[128,8192]{1,0:T(8,128)(2,1)}) %all-gather.5.cloned.1.call-update) | async-done | bytes 2097168 | tf_op jit(solution)/shard_map/all_gather | solution.py:110
  90.4 1.4 slice_convert_fusion
  94.4 2.4 slice_convert_fusion.2
  97.4 1.2 pad_maximum_fusion
  98.8 62.2 %all-to-all-done = bf16[8,128,2048]{2,1,0:T(8,128)(2,1)} async-done(((bf16[8,128,2048]{2,1,0:T(8,128)(2,1)}), bf16[8,128,2048]{2,1,0:T(8,128)(2,1)}, u32[]{:S(2)}, u32[]{:S(2)}) %all-to-all-start) | async-done | bytes 4194336 | tf_op jit(solution)/shard_map/all_to_all | solution.py:16
  161.0 3.8 copy.103
  164.7 5.1 fusion
  169.9 18.5 %all-gather.7.cloned.1.call-done = bf16[1024,2048]{0,1:T(8,128)(2,1)} async-done(((bf16[128,2048]{0,1:T(8,128)(2,1)}), bf16[1024,2048]{0,1:T(8,128)(2,1)}) %all-gather.7.cloned.1.call-update) | async-done | bytes 4194320 | tf_op jit(solution)/shard_map/all_gather | solution.py:145
  188.3 7.2 %fusion.2 = f32[8,128,2,256]{3,1,2,0:T(8,128)S(1)} fusion(bf16[1024,8,256,1]{0,2,3,1:T(8,128)(2,1)} %bitcast.101, f32[8,1024,128,2]{2,1,3,0:T(8,128)} %get-tuple-element.27, pred[128,1024]{0,1:T(8,128)(4,1)} %compare_and_fusion), kind=kOutput, calls=%fused_computation.4 | convolution fusion | flops 1082130432 | bytes 14811136 | tf_op jit(solution)/shard_map/nkjp,pkd->nkjd/dot_general | solution.py:63
  195.5 1.4 copy.137
  197.6 2.9 copy.86
  200.5 2.9 copy.87
  203.7 3.3 fusion.20
  207.0 1.2 copy.96
  208.9 2.8 broadcast_multiply_fusion
  211.7 4.0 mul.269
  215.7 1.3 add.147
  217.0 64.7 %psum.15 = f32[128,16]{0,1:T(8,128)S(1)} all-reduce(f32[128,16]{0,1:T(8,128)S(1)} %bitcast.99), channel_id=1, replica_groups=mesh['grp'=8,'tp'=32] {'tp'}, use_global_device_ids=true, to_apply=%region_8.9 | all-reduce | flops 2048 | bytes 16384 | tf_op jit(solution)/shard_map/psum | solution.py:166
  281.7 37.9 %all-reduce.6.cloned.1.call-done = f32[128,4096]{1,0:T(8,128)} async-done(((f32[128,4096]{1,0:T(8,128)}), f32[128,4096]{1,0:T(8,128)}) %all-reduce.6.cloned.1.call-update) | async-done | bytes 2097168 | tf_op jit(solution)/shard_map/psum | solution.py:166
  320.7 1.6 fusion.78
  323.6 115.3 %all-reduce.8.cloned.1.call-done = f32[128,3584]{1,0:T(8,128)} async-done(((f32[128,3584]{1,0:T(8,128)}), f32[128,3584]{1,0:T(8,128)}) %all-reduce.8.cloned.1.call-update) | async-done | bytes 1835024
  441.2 28.2 %all-gather.1 = bf16[32,4,3584]{2,1,0:T(4,128)(2,1)} all-gather(bf16[1,4,3584]{2,1,0:T(4,128)(2,1)S(1)} %fusion.51), channel_id=1, replica_groups=mesh['grp'=8,'tp'=32] {'tp'}, dimensions={0}, use_global_device_ids=true | all-gather | bytes 946176 | tf_op jit(solution)/shard_map/all_gather | solution.py:198
  469.5 1.7 reshape.289
  471.1 2.7 convolution_bitcast_fusion
  473.8 1.4 convolution_convert_fusion
  475.3 112.7 %all-reduce.10.cloned.1.call-done = bf16[128,3584]{1,0:T(8,128)(2,1)} async-done(((bf16[128,3584]{1,0:T(8,128)(2,1)}), bf16[128,3584]{1,0:T(8,128)(2,1)}) %all-reduce.10.cloned.1.call-update) | async-done | bytes 917520
  589.0 1.5 fusion.47
  (88 shorter events, 16.2 us)
Async XLA Ops:
  6.5 467.3 %copy-start = (bf16[256,3584]{1,0:T(8,128)(2,1)S(1)}, bf16[256,3584]{1,0:T(8,128)(2,1)}, u32[]{:S(2)}) copy-start(bf16[256,3584]{1,0:T(8,128)(2,1)} %param.19) | copy-start | bytes 5505028
  6.5 33.5 %copy-start.1 = (bf16[128,2048]{1,0:T(8,128)(2,1)S(1)}, bf16[128,2048]{1,0:T(8,128)(2,1)}, u32[]{:S(2)}) copy-start(bf16[128,2048]{1,0:T(8,128)(2,1)} %param.20) | copy-start | bytes 1572868
  6.5 83.9 %all-gather.5.cloned.1.call-start = ((), (), s32[]{:S(2)}) async-start(), calls=%async_computation.1 | async-start | bytes 2162688 | tf_op jit(solution)/shard_map/all_gather | solution.py:110
  40.4 2.0 copy-start.2
  42.4 8.4 %copy-start.6 = (bf16[128,2048]{1,0:T(8,128)(2,1)S(1)}, bf16[128,2048]{1,0:T(8,128)(2,1)}, u32[]{:S(2)}) copy-start(bf16[128,2048]{1,0:T(8,128)(2,1)} %param.21) | copy-start | bytes 1572868
  42.4 9.7 %copy-start.12 = (s32[128]{0:T(128)S(1)}, s32[128]{0:T(128)}, u32[]{:S(2)}) copy-start(s32[128]{0:T(128)} %param.27) | copy-start | bytes 1540
  42.4 9.8 %copy-start.9 = (s32[80]{0:T(128)S(1)}, s32[80]{0:T(128)}, u32[]{:S(2)}) copy-start(s32[80]{0:T(128)} %param.25) | copy-start | bytes 964
  42.4 9.8 %copy-start.10 = (s32[80]{0:T(128)S(1)}, s32[80]{0:T(128)}, u32[]{:S(2)}) copy-start(s32[80]{0:T(128)} %param.24) | copy-start | bytes 964
  42.4 10.0 %copy-start.11 = (s32[128]{0:T(128)S(1)}, s32[128]{0:T(128)}, u32[]{:S(2)}) copy-start(s32[128]{0:T(128)} %param.26) | copy-start | bytes 1540
  42.4 118.5 %all-to-all-start = ((bf16[8,128,2048]{2,1,0:T(8,128)(2,1)}), bf16[8,128,2048]{2,1,0:T(8,128)(2,1)}, u32[]{:S(2)}, u32[]{:S(2)}) async-start(bf16[8,128,2048]{2,1,0:T(8,128)(2,1)} %bitcast.85), calls=%async_computation | async-start | bytes 8388608 | tf_op jit(solution)/shard_map/all_to_all | solution.py:16
  50.8 137.6 %all-gather.7.cloned.1.call-start = ((), (), s32[]{:S(2)}) async-start(), calls=%async_computation.2 | async-start | bytes 4718592 | tf_op jit(solution)/shard_map/all_gather | solution.py:145
  51.8 267.7 %all-reduce.6.cloned.1.call-start = ((), (), s32[]{:S(2)}) async-start(), calls=%async_computation.3 | async-start | bytes 4194304 | tf_op jit(solution)/shard_map/psum | solution.py:166
  92.5 1.2 copy-start.13
  96.8 1.8 copy-start.4
  161.0 3.8 copy-start.8
  203.4 5.1 copy-start.3
  203.4 235.5 %all-reduce.8.cloned.1.call-start = ((), (), s32[]{:S(2)}) async-start(), calls=%async_computation.4 | async-start | bytes 3670016
  208.9 111.8 %copy-start.5 = (bf16[128,3584]{1,0:T(8,128)(2,1)S(1)}, bf16[128,3584]{1,0:T(8,128)(2,1)}, u32[]{:S(2)}) copy-start(bf16[128,3584]{1,0:T(8,128)(2,1)} %param.17) | copy-start | bytes 2752516
  211.6 110.7 %copy-start.14 = (u32[256]{0:T(256)S(1)}, u32[256]{0:T(256)}, u32[]{:S(2)}) copy-start(u32[256]{0:T(256)} %constant.96) | copy-start | bytes 3076
  211.7 228.4 %copy-start.7 = (bf16[4,3584]{1,0:T(4,128)(2,1)S(1)}, bf16[4,3584]{1,0:T(4,128)(2,1)}, u32[]{:S(2)}) copy-start(bf16[4,3584]{1,0:T(4,128)(2,1)} %param.14) | copy-start | bytes 86020
  322.3 265.7 %all-reduce.10.cloned.1.call-start = ((), (), s32[]{:S(2)}) async-start(), calls=%async_computation.5 | async-start | bytes 1835008
Sparse Core Ops, SparseCore 0:
  40.2 50.2 all-gather.4
  92.1 96.1 all-gather.6
  203.5 115.9 all-reduce.5
  322.7 116.2 all-reduce.7
  475.4 112.5 all-reduce.9
